TPU v7x, 32 devices: a whole 2x2x4 slice. The times are simulated.
32 devices in a mesh: wa: 8 (over y, x, core), vert: 4 (over z).
Axes of the slice: x: 2, y: 2, z: 4, core: 2. Of those that a mesh axis runs over, the one named last changes fastest.
Arguments:
- spectra: bfloat16 [640, 2, 8, 1288], P('wa', None, 'vert'), may hold values from -0.4375 to 0.4375
- legendre: bfloat16 [640, 1288, 32], P('wa'), may hold values from -0.15625 to 0.15625
- pair_waves: int32 [640], replicated, may hold values from 0 to 639, each once
- points: int32 [64], P('wa'), may hold values from 20 to 5136, as said below
Outputs:
- gridded: float32 [64, 8, 5152], P('wa', None, 'vert')
Inputs may be any that keep to these rules, and one draw needn't show every extreme that they name: Pair slot p holds wavenumbers pair_waves[p] and 1279 - pair_waves[p]; every value of 0 to 639 appears once. Each count is 20 plus four times a whole number; latitude 64 - 1 - i has as many points as latitude i.
All inputs are finite; a program needn't handle non-finite values.
Results may differ from a plain program's by a relative error of at most 0.0037.
Values may be sent and summed in bfloat16 or wider, within the bound.
A program may use at most 128 MiB of HBM per device.

v0:
```python
import functools
import math

import jax
import jax.numpy as jnp
from jax import lax
from jax.experimental import pallas as pl
from jax.experimental.pallas import tpu as pltpu
from jax.sharding import PartitionSpec as P

M = 1280
LANES = 128
SIN_PI = (
    math.pi,
    -math.pi**3 / 6,
    math.pi**5 / 120,
    -math.pi**7 / 5040,
    math.pi**9 / 362880,
    -math.pi**11 / 39916800,
    math.pi**13 / 6227020800,
)

COS_PI = (
    1.0,
    -math.pi**2 / 2,
    math.pi**4 / 24,
    -math.pi**6 / 720,
    math.pi**8 / 40320,
    -math.pi**10 / 3628800,
    math.pi**12 / 479001600,
)


def legendre_kernel(pair_block, bounds_ref, spectra_ref, legendre_ref, out_ref, scratch):
    step = pl.program_id(0)
    parts, fields, padded = spectra_ref.shape[1:]
    half = parts * fields
    heights = legendre_ref.shape[1]
    shape = (2 * half, padded)
    column = lax.broadcasted_iota(jnp.int32, shape, 1)
    plain = lax.broadcasted_iota(jnp.int32, shape, 0) < half
    alternating = jnp.where(plain | (column % 2 == 0), 1.0, -1.0)
    for i in range(pair_block):
        pair = step * pair_block + i
        boundary = M - bounds_ref[pair]
        flip = jnp.where(boundary % 2 == 0, 1.0, -1.0)
        rows = [spectra_ref[i, part].astype(jnp.float32) for part in range(parts)]
        signed = jnp.concatenate(rows + rows, axis=0) * alternating
        first = jnp.where(column < boundary, signed, 0.0)
        second = jnp.where((column >= boundary) & (column < M + 1), signed, 0.0)
        second = second * jnp.where(plain, 1.0, flip)
        masked = jnp.concatenate([first, second], axis=0).astype(jnp.bfloat16)
        scratch[pair, :, 0:heights] = lax.dot_general(
            masked,
            legendre_ref[i],
            (((1,), (1,)), ((), ())),
            preferred_element_type=jnp.float32,
        )

    @pl.when(step == pl.num_programs(0) - 1)
    def _():
        pairs = scratch.shape[0]
        blocks, _, lats, _ = out_ref.shape
        for sign in range(2):
            for row in range(half):
                halves = []
                for part in range(2):
                    picked = scratch[:, (part * 2 + sign) * half + row, :]
                    halves.append(jnp.transpose(picked)[:heights])
                both = jnp.concatenate(halves, axis=1).astype(jnp.bfloat16)
                for b in range(blocks // 2):
                    target = b if sign == 0 else blocks - 1 - b
                    out_ref[target, row] = both[b * lats : (b + 1) * lats]


def legendre_step(spectra, legendre, bounds, blocks):
    pairs, parts, fields, padded = spectra.shape
    heights = legendre.shape[1]
    block = 8 if pairs % 8 == 0 else 4
    lats = 2 * heights // blocks
    return pl.pallas_call(
        functools.partial(legendre_kernel, block),
        out_shape=jax.ShapeDtypeStruct((blocks, parts * fields, lats, 2 * pairs), jnp.bfloat16),
        grid=(pairs // block,),
        in_specs=[
            pl.BlockSpec(memory_space=pltpu.SMEM),
            pl.BlockSpec((block, parts, fields, padded), lambda i: (i, 0, 0, 0)),
            pl.BlockSpec((block, heights, padded), lambda i: (i, 0, 0)),
        ],
        out_specs=pl.BlockSpec((blocks, parts * fields, lats, 2 * pairs), lambda i: (0, 0, 0, 0)),
        scratch_shapes=[
            pltpu.VMEM((pairs, 4 * parts * fields, max(heights, LANES)), jnp.float32)
        ],
        name="legendre",
    )(bounds, spectra, legendre)


def trig(wave, offset, length, inverse):
    product = wave * offset
    turns = (product - jnp.round(product * inverse) * length) * inverse
    square = turns * turns
    sine = jnp.float32(SIN_PI[-1])
    for term in SIN_PI[-2::-1]:
        sine = sine * square + term
    sine = sine * turns
    cosine = jnp.float32(COS_PI[-1])
    for term in COS_PI[-2::-1]:
        cosine = cosine * square + term
    return 1.0 - 2.0 * sine * sine, 2.0 * sine * cosine


def gather_rows(arrived, fields_ref):
    columns, blocks, groups, lats, waves = arrived.shape
    half = groups // 2
    for v in range(columns):
        for g in range(groups):
            pieces = [arrived[v, w, g].astype(jnp.float32) for w in range(blocks)]
            fields_ref[:, g // half, v * half + g % half, :] = jnp.concatenate(pieces, axis=1)


def tables_of(wave, length, inverse, table_ref):
    row = lax.broadcasted_iota(jnp.int32, (8, 1), 0).astype(jnp.float32)
    fine_cos, fine_sin = trig(wave, row, length, inverse)
    for top in range(LANES // 64):
        coarse_cos, coarse_sin = trig(wave, 64 * top + 8 * row, length, inverse)
        for pair in range(4):
            cosines, sines = [], []
            for a in (2 * pair, 2 * pair + 1):
                c, s = coarse_cos[a : a + 1], coarse_sin[a : a + 1]
                cosines.append(c * fine_cos - s * fine_sin)
                sines.append(-(s * fine_cos + c * fine_sin))
            at = 64 * top + 16 * pair
            table_ref[at : at + 16, 0:M] = jnp.concatenate(cosines, axis=0).astype(jnp.bfloat16)
            table_ref[at : at + 16, M : 2 * M] = jnp.concatenate(sines, axis=0).astype(jnp.bfloat16)


def synthesis(wave, count, first_point, fields_ref, table_ref, left_ref, out_ref):
    length = count.astype(jnp.float32)
    inverse = 1.0 / length
    tables_of(wave, length, inverse, table_ref)
    fields, points = out_ref.shape
    weight = jnp.where(wave == 0, 1.0, jnp.where(2 * wave < length, 2.0, 0.0))
    row = lax.broadcasted_iota(jnp.int32, (8, 1), 0).astype(jnp.float32)
    start = first_point.astype(jnp.float32)
    blocks = pl.cdiv(points, LANES)
    for block in range(blocks):
        if block % 8 == 0:
            block_cos, block_sin = trig(wave, start + LANES * (block + row), length, inverse)
            block_cos, block_sin = block_cos * weight, block_sin * weight
        c = block_cos[block % 8 : block % 8 + 1]
        s = block_sin[block % 8 : block % 8 + 1]
        real, imag = fields_ref[0], fields_ref[1]
        at = block * fields
        left_ref[at : at + fields, 0:M] = (real * c - imag * s).astype(jnp.bfloat16)
        left_ref[at : at + fields, M : 2 * M] = (real * s + imag * c).astype(jnp.bfloat16)
    product = lax.dot_general(
        left_ref[...],
        table_ref[...],
        (((1,), (1,)), ((), ())),
        preferred_element_type=jnp.float32,
    )
    lane = lax.broadcasted_iota(jnp.int32, (fields, LANES), 1)
    for block in range(blocks):
        width = min(LANES, points - block * LANES)
        values = product[block * fields : (block + 1) * fields]
        inside = first_point + block * LANES + lane < count
        out_ref[:, block * LANES : block * LANES + width] = jnp.where(inside, values, 0.0)[:, :width]


def fourier_kernel(points_ref, waves_ref, arrived, out_ref, fields_ref, table_ref, left_ref):
    lats, _, points = out_ref.shape
    blocks = arrived.shape[1]
    first_point = lax.axis_index("vert") * points
    southern = lax.axis_index("wa") >= blocks // 2
    wave = waves_ref[...]
    gather_rows(arrived, fields_ref)

    def one(i, carry):
        lat = jnp.where(southern, lats - 1 - i, i)
        synthesis(
            wave, points_ref[lat], first_point, fields_ref.at[i], table_ref, left_ref, out_ref.at[lat]
        )
        return carry

    lax.fori_loop(0, lats, one, 0)


def fourier_step(arrived, waves, points, points_device):
    columns, blocks, groups, lats, _ = arrived.shape
    fields = columns * groups // 2
    rows = pl.cdiv(points_device, LANES) * fields
    return pl.pallas_call(
        fourier_kernel,
        out_shape=jax.ShapeDtypeStruct((lats, fields, points_device), jnp.float32),
        in_specs=[
            pl.BlockSpec(memory_space=pltpu.SMEM),
            pl.BlockSpec(memory_space=pltpu.VMEM),
            pl.BlockSpec(memory_space=pltpu.VMEM),
        ],
        out_specs=pl.BlockSpec(memory_space=pltpu.VMEM),
        scratch_shapes=[
            pltpu.VMEM((lats, 2, fields, M), jnp.float32),
            pltpu.VMEM((LANES, 2 * M), jnp.bfloat16),
            pltpu.VMEM((rows, 2 * M), jnp.bfloat16),
        ],
        name="fourier",
    )(points, waves, arrived)


def body(spectra, legendre, pair_waves, points):
    blocks, columns = lax.axis_size("wa"), lax.axis_size("vert")
    pair_count = legendre.shape[0]
    bounds = lax.dynamic_slice_in_dim(pair_waves, lax.axis_index("wa") * pair_count, pair_count)
    lower = pair_waves.reshape(blocks, 1, pair_count)
    waves = jnp.concatenate([lower, M - 1 - lower], axis=1).reshape(1, -1).astype(jnp.float32)
    step_length = 8 * columns
    points_device = 8 * ((4 * M + 16 + step_length - 1) // step_length)
    sent = legendre_step(spectra, jnp.swapaxes(legendre, 1, 2), bounds, blocks)
    banded = lax.all_to_all(sent, "wa", split_axis=0, concat_axis=0, tiled=True)
    spread = jnp.broadcast_to(banded[None], (columns,) + banded.shape)
    arrived = lax.all_to_all(spread, "vert", split_axis=0, concat_axis=0, tiled=True)
    return fourier_step(arrived, waves, points, points_device)


def solution(mesh):
    in_specs = (P("wa", None, "vert", None), P("wa", None, None), P(), P("wa"))
    out_specs = P("wa", None, "vert")
    return jax.shard_map(body, mesh=mesh, in_specs=in_specs, out_specs=out_specs, check_vma=False)
```

profile of v0, /device:TPU:0, one launch (start us, length us, event | category | flops | bytes accessed | tf_op | source)
XLA Modules:
  0.0 50.5 jit_solution(15488140409002241642)
XLA Ops:
  0.0 0.0 copy-start.1
  0.0 1.4 %dynamic_slice.3.bounds_ref = s32[80]{0:T(128)} dynamic-slice(s32[640]{0:T(1024)} %param.6, s32[]{:T(128)S(6)} %select_n.3), dynamic_slice_sizes={80} | dynamic-slice | bytes 644 | tf_op jit(solution)/shard_map/dynamic_slice | solution.py:213
  1.4 9.1 %legendre.1 = bf16[8,4,8,160]{3,2,1,0:T(8,128)(2,1)} custom-call(s32[80]{0:T(128)} %dynamic_slice.3.bounds_ref, bf16[80,2,2,1288]{3,2,1,0:T(2,128)(2,1)} %spectra_ref.1, bf16[80,32,1288]{2,1,0:T(8,128)(2,1)} %bitcast.1), custom_call_target="tpu_custom_call" | custom-call | tf_op jit(solution)/shard_map/legendre/pallas_call | solution.py:81
  10.5 10.7 %all_to_all.10 = bf16[8,4,8,160]{3,2,1,0:T(8,128)(2,1)S(1)} all-to-all(bf16[8,4,8,160]{3,2,1,0:T(8,128)(2,1)} %legendre.1), channel_id=1, replica_groups=mesh['wa'=8,'vert'=4] {'wa'}, dimensions={0} | all-to-all | bytes 163840 | tf_op jit(solution)/shard_map/all_to_all | solution.py:219
  21.2 0.9 %broadcast_in_dim.2 = bf16[4,8,4,8,160]{4,3,2,1,0:T(8,128)(2,1)} broadcast(bf16[8,4,8,160]{3,2,1,0:T(8,128)(2,1)S(1)} %all_to_all.10), dimensions={1,2,3,4} | broadcast | bytes 409600 | tf_op jit(solution)/shard_map/broadcast_in_dim | solution.py:220
  22.0 4.9 %all-to-all-start.1 = ((bf16[4,8,4,8,160]{4,3,2,1,0:T(8,128)(2,1)}), bf16[4,8,4,8,160]{4,3,2,1,0:T(8,128)(2,1)S(1)}, u32[]{:S(2)}, u32[]{:S(2)}) async-start(bf16[4,8,4,8,160]{4,3,2,1,0:T(8,128)(2,1)} %broadcast_in_dim.2), calls=%async_computation.1 | async-start | bytes 1048576 | tf_op jit(solution)/shard_map/all_to_all | solution.py:221
  26.9 0.0 copy-done.1
  26.9 0.1 reshape.30
  27.0 0.7 %convert_element_type.6.waves_ref = f32[1,1280]{1,0:T(1,128)} reshape(f32[8,2,80]{2,1,0:T(2,128)S(1)} %add_convert_fusion) | data formatting | bytes 10240 | tf_op jit(solution)/shard_map/convert_element_type | solution.py:215
  27.7 13.4 %all-to-all-done.1.arrived = bf16[4,8,4,8,160]{4,3,2,1,0:T(8,128)(2,1)S(1)} async-done(((bf16[4,8,4,8,160]{4,3,2,1,0:T(8,128)(2,1)}), bf16[4,8,4,8,160]{4,3,2,1,0:T(8,128)(2,1)S(1)}, u32[]{:S(2)}, u32[]{:S(2)}) %all-to-all-start.1) | async-done | bytes 327712 | tf_op jit(solution)/shard_map/all_to_all | solution.py:221
  41.1 0.0 copy-start
  41.1 0.8 %copy-done = bf16[4,8,4,8,160]{4,3,2,1,0:T(8,128)(2,1)} copy-done((bf16[4,8,4,8,160]{4,3,2,1,0:T(8,128)(2,1)}, bf16[4,8,4,8,160]{4,3,2,1,0:T(8,128)(2,1)S(1)}, u32[]{:S(2)}) %copy-start) | copy-done | bytes 327704
  41.9 8.6 %fourier.1 = f32[8,8,1288]{2,1,0:T(8,128)} custom-call(s32[8]{0:T(128)} %points_ref.1, f32[1,1280]{1,0:T(1,128)} %convert_element_type.6.waves_ref, bf16[4,8,4,8,160]{4,3,2,1,0:T(8,128)(2,1)} %copy-done), custom_call_target="tpu_custom_call" | custom-call | tf_op jit(solution)/shard_map/fourier/pallas_call | solution.py:192
  (2 shorter events, 0.0 us)
Async XLA Ops:
  0.0 26.9 %copy-start.1 = (s32[640]{0:T(1024)S(1)}, s32[640]{0:T(1024)}, u32[]{:S(2)}) copy-start(s32[640]{0:T(1024)} %param.6) | copy-start | bytes 7684
  22.0 19.1 %all-to-all-start.1 = ((bf16[4,8,4,8,160]{4,3,2,1,0:T(8,128)(2,1)}), bf16[4,8,4,8,160]{4,3,2,1,0:T(8,128)(2,1)S(1)}, u32[]{:S(2)}, u32[]{:S(2)}) async-start(bf16[4,8,4,8,160]{4,3,2,1,0:T(8,128)(2,1)} %broadcast_in_dim.2), calls=%async_computation.1 | async-start | bytes 1048576 | tf_op jit(solution)/shard_map/all_to_all | solution.py:221
  41.1 0.8 %copy-start = (bf16[4,8,4,8,160]{4,3,2,1,0:T(8,128)(2,1)}, bf16[4,8,4,8,160]{4,3,2,1,0:T(8,128)(2,1)S(1)}, u32[]{:S(2)}) copy-start(bf16[4,8,4,8,160]{4,3,2,1,0:T(8,128)(2,1)S(1)} %all-to-all-done.1.arrived) | copy-start | bytes 983044
where the time goes:
time: 50.9 us; the launch traced here: 50.5 us
  Pallas kernels  17.7 us (35%)
  waiting for transfers between devices  13.4 us (26%)
  blocking collectives  10.7 us (21%)
  starting transfers between devices  4.87 us (10%)
  local copies, waits for them, and re-layouts  3.78 us (7%)
    all_to_all x1, waiting for transfers between devices, body(): lax.all_to_all(spread, 'vert', split_axis=0, concat_axis=0, tiled=True)  13.4 us
    all_to_all x1, blocking collectives, body(): banded = lax.all_to_all(sent, 'wa', split_axis=0, concat_axis=0, tiled=True)  10.7 us
    pallas_call x1, Pallas kernels, legendre_step(): pl.pallas_call(functools.partial(legendre_kernel, block), out_shape=jax.S...  9.13 us
    pallas_call x1, Pallas kernels, fourier_step(): pl.pallas_call(fourier_kernel, out_shape=jax.ShapeDtypeStruct((lats, fiel...  8.55 us
    all_to_all x1, starting transfers between devices, body(): lax.all_to_all(spread, 'vert', split_axis=0, concat_axis=0, tiled=True)  4.87 us
    dynamic_slice x1, local copies, waits for them, and re-layouts, body(): lax.dynamic_slice_in_dim(pair_waves, lax.axis_index('wa') * pair_count, p...  1.37 us
  transfers between devices with their start and end apart: 1, of which 1 were waited for; matrix products, arithmetic and copies ran while one was open for 2% of the time, Pallas kernels for 0%

commit v1 on v0

--- a/solution.py
+++ b/solution.py
@@ -10,6 +10,7 @@
 
 M = 1280
 LANES = 128
+MESH = pl.DeviceIdType.MESH
 SIN_PI = (
     math.pi,
     -math.pi**3 / 6,
@@ -29,6 +30,18 @@
     -math.pi**10 / 3628800,
     math.pi**12 / 479001600,
 )
+
+
+def packing(waves, groups):
+    full, rest = divmod(waves, LANES)
+    per_slot = LANES // rest if rest else 1
+    slots = full * groups + (-(-groups // per_slot) if rest else 0)
+    return full, rest, per_slot, slots
+
+
+def packed_order(waves):
+    cut = waves.shape[1] // LANES * LANES
+    return jnp.concatenate([waves[:, :cut].reshape(-1), waves[:, cut:].reshape(-1)])
 
 
 def legendre_kernel(pair_block, bounds_ref, spectra_ref, legendre_ref, out_ref, scratch):
@@ -59,18 +72,33 @@
 
     @pl.when(step == pl.num_programs(0) - 1)
     def _():
-        pairs = scratch.shape[0]
         blocks, _, lats, _ = out_ref.shape
+        full, rest, per_slot, _ = packing(2 * scratch.shape[0], half)
         for sign in range(2):
+            rows = []
             for row in range(half):
                 halves = []
                 for part in range(2):
                     picked = scratch[:, (part * 2 + sign) * half + row, :]
                     halves.append(jnp.transpose(picked)[:heights])
-                both = jnp.concatenate(halves, axis=1).astype(jnp.bfloat16)
+                rows.append(jnp.concatenate(halves, axis=1))
+            slots = [
+                rows[row][:, chunk * LANES : (chunk + 1) * LANES]
+                for chunk in range(full)
+                for row in range(half)
+            ]
+            if rest:
+                for at in range(0, half, per_slot):
+                    pieces = [row[:, full * LANES :] for row in rows[at : at + per_slot]]
+                    spare = LANES - rest * len(pieces)
+                    if spare:
+                        pieces.append(jnp.zeros((heights, spare), jnp.float32))
+                    slots.append(jnp.concatenate(pieces, axis=1))
+            for slot, values in enumerate(slots):
+                values = values.astype(jnp.bfloat16)
                 for b in range(blocks // 2):
                     target = b if sign == 0 else blocks - 1 - b
-                    out_ref[target, row] = both[b * lats : (b + 1) * lats]
+                    out_ref[target, slot] = values[b * lats : (b + 1) * lats]
 
 
 def legendre_step(spectra, legendre, bounds, blocks):
@@ -78,16 +106,18 @@
     heights = legendre.shape[1]
     block = 8 if pairs % 8 == 0 else 4
     lats = 2 * heights // blocks
+    slots = packing(2 * pairs, parts * fields)[3]
+    result = (blocks, slots, lats, LANES)
     return pl.pallas_call(
         functools.partial(legendre_kernel, block),
-        out_shape=jax.ShapeDtypeStruct((blocks, parts * fields, lats, 2 * pairs), jnp.bfloat16),
+        out_shape=jax.ShapeDtypeStruct(result, jnp.bfloat16),
         grid=(pairs // block,),
         in_specs=[
             pl.BlockSpec(memory_space=pltpu.SMEM),
             pl.BlockSpec((block, parts, fields, padded), lambda i: (i, 0, 0, 0)),
             pl.BlockSpec((block, heights, padded), lambda i: (i, 0, 0)),
         ],
-        out_specs=pl.BlockSpec((blocks, parts * fields, lats, 2 * pairs), lambda i: (0, 0, 0, 0)),
+        out_specs=pl.BlockSpec(result, lambda i: (0, 0, 0, 0)),
         scratch_shapes=[
             pltpu.VMEM((pairs, 4 * parts * fields, max(heights, LANES)), jnp.float32)
         ],
@@ -109,12 +139,21 @@
     return 1.0 - 2.0 * sine * sine, 2.0 * sine * cosine
 
 
-def gather_rows(arrived, fields_ref):
-    columns, blocks, groups, lats, waves = arrived.shape
+def gather_rows(arrived, fields_ref, groups, waves):
+    columns, blocks, _, lats, _ = arrived.shape
+    full, rest, per_slot, _ = packing(waves, groups)
     half = groups // 2
     for v in range(columns):
         for g in range(groups):
-            pieces = [arrived[v, w, g].astype(jnp.float32) for w in range(blocks)]
+            pieces = [
+                arrived[v, w, chunk * groups + g].astype(jnp.float32)
+                for w in range(blocks)
+                for chunk in range(full)
+            ]
+            if rest:
+                slot, at = full * groups + g // per_slot, g % per_slot * rest
+                ends = [arrived[v, w, slot].astype(jnp.float32) for w in range(blocks)]
+                pieces += [end[:, at : at + rest] for end in ends]
             fields_ref[:, g // half, v * half + g % half, :] = jnp.concatenate(pieces, axis=1)
 
 
@@ -137,7 +176,6 @@
 def synthesis(wave, count, first_point, fields_ref, table_ref, left_ref, out_ref):
     length = count.astype(jnp.float32)
     inverse = 1.0 / length
-    tables_of(wave, length, inverse, table_ref)
     fields, points = out_ref.shape
     weight = jnp.where(wave == 0, 1.0, jnp.where(2 * wave < length, 2.0, 0.0))
     row = lax.broadcasted_iota(jnp.int32, (8, 1), 0).astype(jnp.float32)
@@ -167,59 +205,187 @@
         out_ref[:, block * LANES : block * LANES + width] = jnp.where(inside, values, 0.0)[:, :width]
 
 
-def fourier_kernel(points_ref, waves_ref, arrived, out_ref, fields_ref, table_ref, left_ref):
+def fourier_kernel(
+    groups, points_ref, waves_ref, sent, out_ref,
+    arrived, fields_ref, tables_ref, left_ref,
+    own_sem, send_band, recv_band, send_level, recv_level,
+):
     lats, _, points = out_ref.shape
-    blocks = arrived.shape[1]
-    first_point = lax.axis_index("vert") * points
-    southern = lax.axis_index("wa") >= blocks // 2
+    columns, blocks = arrived.shape[:2]
+    me, level = lax.axis_index("wa"), lax.axis_index("vert")
+    barrier = pltpu.get_barrier_semaphore()
+
+    def greet_band(d, carry):
+        pl.semaphore_signal(
+            barrier, inc=1, device_id=(lax.rem(me + d, blocks), level), device_id_type=MESH
+        )
+        return carry
+
+    def greet_level(e, carry):
+        pl.semaphore_signal(
+            barrier, inc=1, device_id=(me, lax.rem(level + e, columns)), device_id_type=MESH
+        )
+        return carry
+
+    lax.fori_loop(1, blocks, greet_band, 0)
+    lax.fori_loop(1, columns, greet_level, 0)
+    pl.semaphore_wait(barrier, blocks + columns - 2)
+
+    def band_copy(d):
+        target = lax.rem(me + d, blocks)
+        return pltpu.make_async_remote_copy(
+            src_ref=sent.at[target],
+            dst_ref=arrived.at[level, me],
+            send_sem=send_band.at[d],
+            recv_sem=recv_band.at[d],
+            device_id=(target, level),
+            device_id_type=MESH,
+        )
+
+    def band_arrival(d):
+        source = lax.rem(me + blocks - d, blocks)
+        return pltpu.make_async_remote_copy(
+            src_ref=sent.at[source],
+            dst_ref=arrived.at[level, source],
+            send_sem=send_band.at[d],
+            recv_sem=recv_band.at[d],
+            device_id=(source, level),
+            device_id_type=MESH,
+        )
+
+    def level_copy(d, e):
+        source = lax.rem(me + blocks - d, blocks)
+        return pltpu.make_async_remote_copy(
+            src_ref=arrived.at[level, source],
+            dst_ref=arrived.at[level, source],
+            send_sem=send_level.at[d, e],
+            recv_sem=recv_level.at[d, e],
+            device_id=(me, lax.rem(level + e, columns)),
+            device_id_type=MESH,
+        )
+
+    def level_arrival(d, e):
+        source, column = lax.rem(me + blocks - d, blocks), lax.rem(level + columns - e, columns)
+        return pltpu.make_async_remote_copy(
+            src_ref=arrived.at[column, source],
+            dst_ref=arrived.at[column, source],
+            send_sem=send_level.at[d, e],
+            recv_sem=recv_level.at[d, e],
+            device_id=(me, column),
+            device_id_type=MESH,
+        )
+
+    def start_band(d, carry):
+        band_copy(d).start()
+        return carry
+
+    own = pltpu.make_async_copy(sent.at[me], arrived.at[level, me], own_sem)
+    own.start()
+    lax.fori_loop(1, blocks, start_band, 0)
+
     wave = waves_ref[...]
-    gather_rows(arrived, fields_ref)
+    southern = me >= blocks // 2
+
+    def lat_of(i):
+        return jnp.where(southern, lats - 1 - i, i)
+
+    def make_tables(i, carry):
+        length = points_ref[lat_of(i)].astype(jnp.float32)
+        tables_of(wave, length, 1.0 / length, tables_ref.at[i])
+        return carry
+
+    def start_levels(d):
+        def start_level(e, carry):
+            level_copy(d, e).start()
+            return carry
+
+        lax.fori_loop(1, columns, start_level, 0)
+
+    def forward(d, carry):
+        band_arrival(d).wait_recv()
+        start_levels(d)
+        return carry
+
+    own.wait()
+    start_levels(0)
+    early = lats // 4
+    lax.fori_loop(0, early, make_tables, 0)
+    lax.fori_loop(1, blocks, forward, 0)
+    lax.fori_loop(early, lats, make_tables, 0)
+
+    def finish_level(d, carry):
+        def finish(e, inner):
+            level_arrival(d, e).wait_recv()
+            level_copy(d, e).wait_send()
+            return inner
+
+        return lax.fori_loop(1, columns, finish, carry)
+
+    def finish_band(d, carry):
+        band_copy(d).wait_send()
+        return carry
+
+    lax.fori_loop(0, blocks, finish_level, 0)
+    lax.fori_loop(1, blocks, finish_band, 0)
+    gather_rows(arrived, fields_ref, groups, M // blocks)
 
     def one(i, carry):
-        lat = jnp.where(southern, lats - 1 - i, i)
+        lat = lat_of(i)
         synthesis(
-            wave, points_ref[lat], first_point, fields_ref.at[i], table_ref, left_ref, out_ref.at[lat]
+            wave,
+            points_ref[lat],
+            level * points,
+            fields_ref.at[i],
+            tables_ref.at[i],
+            left_ref,
+            out_ref.at[lat],
         )
         return carry
 
     lax.fori_loop(0, lats, one, 0)
 
 
-def fourier_step(arrived, waves, points, points_device):
-    columns, blocks, groups, lats, _ = arrived.shape
+def fourier_step(sent, waves, points, points_device, groups, columns):
+    blocks, slots, lats, _ = sent.shape
     fields = columns * groups // 2
     rows = pl.cdiv(points_device, LANES) * fields
     return pl.pallas_call(
-        fourier_kernel,
+        functools.partial(fourier_kernel, groups),
         out_shape=jax.ShapeDtypeStruct((lats, fields, points_device), jnp.float32),
         in_specs=[
             pl.BlockSpec(memory_space=pltpu.SMEM),
             pl.BlockSpec(memory_space=pltpu.VMEM),
-            pl.BlockSpec(memory_space=pltpu.VMEM),
+            pl.BlockSpec(memory_space=pl.ANY),
         ],
         out_specs=pl.BlockSpec(memory_space=pltpu.VMEM),
         scratch_shapes=[
+            pltpu.VMEM((columns, blocks, slots, lats, LANES), jnp.bfloat16),
             pltpu.VMEM((lats, 2, fields, M), jnp.float32),
-            pltpu.VMEM((LANES, 2 * M), jnp.bfloat16),
+            pltpu.VMEM((lats, LANES, 2 * M), jnp.bfloat16),
             pltpu.VMEM((rows, 2 * M), jnp.bfloat16),
+            pltpu.SemaphoreType.DMA,
+            pltpu.SemaphoreType.DMA((blocks,)),
+            pltpu.SemaphoreType.DMA((blocks,)),
+            pltpu.SemaphoreType.DMA((blocks, columns)),
+            pltpu.SemaphoreType.DMA((blocks, columns)),
         ],
+        compiler_params=pltpu.CompilerParams(collective_id=0, has_side_effects=True),
         name="fourier",
-    )(points, waves, arrived)
+    )(points, waves, sent)
 
 
 def body(spectra, legendre, pair_waves, points):
     blocks, columns = lax.axis_size("wa"), lax.axis_size("vert")
     pair_count = legendre.shape[0]
     bounds = lax.dynamic_slice_in_dim(pair_waves, lax.axis_index("wa") * pair_count, pair_count)
-    lower = pair_waves.reshape(blocks, 1, pair_count)
-    waves = jnp.concatenate([lower, M - 1 - lower], axis=1).reshape(1, -1).astype(jnp.float32)
+    lower = pair_waves.reshape(blocks, pair_count)
+    waves = packed_order(jnp.concatenate([lower, M - 1 - lower], axis=1))
+    waves = waves.reshape(1, -1).astype(jnp.float32)
     step_length = 8 * columns
     points_device = 8 * ((4 * M + 16 + step_length - 1) // step_length)
     sent = legendre_step(spectra, jnp.swapaxes(legendre, 1, 2), bounds, blocks)
-    banded = lax.all_to_all(sent, "wa", split_axis=0, concat_axis=0, tiled=True)
-    spread = jnp.broadcast_to(banded[None], (columns,) + banded.shape)
-    arrived = lax.all_to_all(spread, "vert", split_axis=0, concat_axis=0, tiled=True)
-    return fourier_step(arrived, waves, points, points_device)
+    groups = spectra.shape[1] * spectra.shape[2]
+    return fourier_step(sent, waves, points, points_device, groups, columns)
 
 
 def solution(mesh):

time: 50.9 us -> 36.4 us (0.72)
  Pallas kernels: 17.7 us -> 31.2 us
  waiting for transfers between devices: 13.4 us -> 0 us
  blocking collectives: 10.7 us -> 0 us
  starting transfers between devices: 4.87 us -> 0 us
  other arithmetic: 0.02 us -> 0.68 us
    pallas_call x1, Pallas kernels: 8.55 us -> 22.1 us  [fourier_step(): pl.pallas_call(functools.partial(fourier_kernel, groups), out_shape=jax.S...]
    all_to_all x1 -> x0, waiting for transfers between devices: 13.4 us -> none  [body(): lax.all_to_all(spread, 'vert', split_axis=0, concat_axis=0, tiled=True)]
    all_to_all x1 -> x0, blocking collectives: 10.7 us -> none  [body(): banded = lax.all_to_all(sent, 'wa', split_axis=0, concat_axis=0, tiled=True)]
    all_to_all x1 -> x0, starting transfers between devices: 4.87 us -> none  [body(): lax.all_to_all(spread, 'vert', split_axis=0, concat_axis=0, tiled=True)]
    unnamed x4 -> x1, local copies, waits for them, and re-layouts: 0.79 us -> 1.74 us
    broadcast_in_dim x1 -> x0, local copies, waits for them, and re-layouts: 0.85 us -> none  [body(): spread = jnp.broadcast_to(banded[None], (columns,) + banded.shape)]
    convert_element_type x1 -> x0, local copies, waits for them, and re-layouts: 0.69 us -> none  [body(): jnp.concatenate([lower, M - 1 - lower], axis=1).reshape(1, -1)]
    reshape x1, local copies, waits for them, and re-layouts: 0.08 us -> 0.76 us  [body(): lower = pair_waves.reshape(blocks, pair_count)]
  transfers between devices with their start and end apart: 1 -> 0, of which waited for: 1 -> 0; matrix products, arithmetic and copies ran while one was open for 2% -> 0% of each run, Pallas kernels for 0% -> 0%
where the time goes in v1:
time: 36.4 us; the launch traced here: 35.9 us
  Pallas kernels  31.2 us (86%)
  local copies, waits for them, and re-layouts  4 us (11%)
  other arithmetic  0.68 us (2%)
    pallas_call x1, Pallas kernels, fourier_step(): pl.pallas_call(functools.partial(fourier_kernel, groups), out_shape=jax.S...  22.1 us
    pallas_call x1, Pallas kernels, legendre_step(): pl.pallas_call(functools.partial(legendre_kernel, block), out_shape=jax.S...  9.17 us
    unnamed x1, local copies, waits for them, and re-layouts  1.74 us
    dynamic_slice x1, local copies, waits for them, and re-layouts, body(): lax.dynamic_slice_in_dim(pair_waves, lax.axis_index('wa') * pair_count, p...  1.35 us
    reshape x1, local copies, waits for them, and re-layouts, body(): lower = pair_waves.reshape(blocks, pair_count)  0.76 us

profile of v1, /device:TPU:0, one launch (start us, length us, event | category | flops | bytes accessed | tf_op | source)
XLA Modules:
  0.0 35.9 jit_solution(5006558997273203302)
XLA Ops:
  0.0 1.3 %dynamic_slice.3.bounds_ref = s32[80]{0:T(128)} dynamic-slice(s32[640]{0:T(1024)} %param.6, s32[]{:T(128)S(6)} %select_n.3), dynamic_slice_sizes={80} | dynamic-slice | bytes 644 | tf_op jit(solution)/shard_map/dynamic_slice | solution.py:380
  1.3 0.8 %reshape.38 = s32[8,80]{1,0:T(8,128)S(1)} reshape(s32[640]{0:T(1024)} %param.6) | data formatting | bytes 5120 | tf_op jit(solution)/shard_map/reshape | solution.py:381
  2.1 0.1 pad_add_fusion
  2.2 0.1 slice.7
  2.3 0.1 concatenate.19
  2.3 0.6 %add_convert_fusion.waves_ref = f32[1,1280]{1,0:T(1,128)} fusion(s32[1,256]{1,0:T(1,128)S(1)} %concatenate.19, s32[1,1024]{1,0:T(1,128)S(1)} %bitcast.3), kind=kLoop, calls=%fused_computation | loop fusion | flops 2560 | bytes 10240 | tf_op jit(solution)/shard_map/convert_element_type | solution.py:383
  2.9 9.2 %legendre.1.sent = bf16[8,5,8,128]{3,2,1,0:T(8,128)(2,1)} custom-call(s32[80]{0:T(128)} %dynamic_slice.3.bounds_ref, bf16[80,2,2,1288]{3,2,1,0:T(2,128)(2,1)} %spectra_ref.1, bf16[80,32,1288]{2,1,0:T(8,128)(2,1)} %bitcast.2), custom_call_target="tpu_custom_call" | custom-call | tf_op jit(solution)/shard_map/legendre/pallas_call | solution.py:111
  12.1 22.1 %fourier.1 = f32[8,8,1288]{2,1,0:T(8,128)} custom-call(s32[8]{0:T(128)} %points_ref.1, f32[1,1280]{1,0:T(1,128)} %add_convert_fusion.waves_ref, bf16[8,5,8,128]{3,2,1,0:T(8,128)(2,1)} %legendre.1.sent), custom_call_target="tpu_custom_call" | custom-call | tf_op jit(solution)/shard_map/fourier/pallas_call | solution.py:352
  34.2 1.7 %copy.6 = f32[8,8,1288]{2,1,0:T(8,128)} copy(f32[8,8,1288]{2,1,0:T(8,128)} %fourier.1) | data formatting | bytes 659456
  (1 shorter events, 0.0 us)

commit v2 on v1

v2 whole, which is shorter than its diff:
```python
import functools
import math

import jax
import jax.numpy as jnp
from jax import lax
from jax.experimental import pallas as pl
from jax.experimental.pallas import tpu as pltpu
from jax.sharding import PartitionSpec as P

M = 1280
LANES = 128
MESH = pl.DeviceIdType.MESH
SIN_PI = (
    math.pi,
    -math.pi**3 / 6,
    math.pi**5 / 120,
    -math.pi**7 / 5040,
    math.pi**9 / 362880,
    -math.pi**11 / 39916800,
    math.pi**13 / 6227020800,
)

COS_PI = (
    1.0,
    -math.pi**2 / 2,
    math.pi**4 / 24,
    -math.pi**6 / 720,
    math.pi**8 / 40320,
    -math.pi**10 / 3628800,
    math.pi**12 / 479001600,
)


def packing(waves, groups):
    full, rest = divmod(waves, LANES)
    per_slot = LANES // rest if rest else 1
    slots = full * groups + (-(-groups // per_slot) if rest else 0)
    return full, rest, per_slot, slots


def packed_order(pairs, blocks):
    count = pairs.shape[1] // blocks
    cut = 2 * count // LANES * LANES
    waves = []
    for block in range(blocks):
        lower = pairs[:, block * count : (block + 1) * count]
        waves.append(jnp.concatenate([lower, M - 1 - lower], axis=1))
    heads = [wave[:, :cut] for wave in waves] if cut else []
    tails = [wave[:, cut:] for wave in waves] if cut < 2 * count else []
    return jnp.concatenate(heads + tails, axis=1)


def legendre_kernel(pair_block, waves_ref, spectra_ref, legendre_ref, out_ref, scratch):
    step = pl.program_id(0)
    parts, fields, padded = spectra_ref.shape[1:]
    half = parts * fields
    heights = legendre_ref.shape[1]
    num_pairs = scratch.shape[0]
    shape = (2 * half, padded)
    column = lax.broadcasted_iota(jnp.int32, shape, 1)
    plain = lax.broadcasted_iota(jnp.int32, shape, 0) < half
    alternating = jnp.where(plain | (column % 2 == 0), 1.0, -1.0)
    for i in range(pair_block):
        pair = step * pair_block + i
        boundary = M - waves_ref[lax.axis_index("wa") * num_pairs + pair]
        flip = jnp.where(boundary % 2 == 0, 1.0, -1.0)
        rows = [spectra_ref[i, part].astype(jnp.float32) for part in range(parts)]
        signed = jnp.concatenate(rows + rows, axis=0) * alternating
        first = jnp.where(column < boundary, signed, 0.0)
        second = jnp.where((column >= boundary) & (column < M + 1), signed, 0.0)
        second = second * jnp.where(plain, 1.0, flip)
        masked = jnp.concatenate([first, second], axis=0).astype(jnp.bfloat16)
        scratch[pair, :, 0:heights] = lax.dot_general(
            masked,
            legendre_ref[i],
            (((1,), (1,)), ((), ())),
            preferred_element_type=jnp.float32,
        )

    @pl.when(step == pl.num_programs(0) - 1)
    def _():
        blocks, _, lats, _ = out_ref.shape
        full, rest, per_slot, _ = packing(2 * scratch.shape[0], half)
        for sign in range(2):
            rows = []
            for row in range(half):
                halves = []
                for part in range(2):
                    picked = scratch[:, (part * 2 + sign) * half + row, :]
                    halves.append(jnp.transpose(picked)[:heights])
                rows.append(jnp.concatenate(halves, axis=1))
            slots = [
                rows[row][:, chunk * LANES : (chunk + 1) * LANES]
                for chunk in range(full)
                for row in range(half)
            ]
            if rest:
                for at in range(0, half, per_slot):
                    pieces = [row[:, full * LANES :] for row in rows[at : at + per_slot]]
                    spare = LANES - rest * len(pieces)
                    if spare:
                        pieces.append(jnp.zeros((heights, spare), jnp.float32))
                    slots.append(jnp.concatenate(pieces, axis=1))
            for slot, values in enumerate(slots):
                values = values.astype(jnp.bfloat16)
                for b in range(blocks // 2):
                    target = b if sign == 0 else blocks - 1 - b
                    out_ref[target, slot] = values[b * lats : (b + 1) * lats]


def legendre_step(spectra, legendre, pair_waves, blocks):
    pairs, parts, fields, padded = spectra.shape
    heights = legendre.shape[1]
    block = 8 if pairs % 8 == 0 else 4
    lats = 2 * heights // blocks
    slots = packing(2 * pairs, parts * fields)[3]
    result = (blocks, slots, lats, LANES)
    return pl.pallas_call(
        functools.partial(legendre_kernel, block),
        out_shape=jax.ShapeDtypeStruct(result, jnp.bfloat16),
        grid=(pairs // block,),
        in_specs=[
            pl.BlockSpec(memory_space=pltpu.SMEM),
            pl.BlockSpec((block, parts, fields, padded), lambda i: (i, 0, 0, 0)),
            pl.BlockSpec((block, heights, padded), lambda i: (i, 0, 0)),
        ],
        out_specs=pl.BlockSpec(result, lambda i: (0, 0, 0, 0)),
        scratch_shapes=[
            pltpu.VMEM((pairs, 4 * parts * fields, max(heights, LANES)), jnp.float32)
        ],
        name="legendre",
    )(pair_waves, spectra, legendre)


def trig(wave, offset, length, inverse):
    product = wave * offset
    turns = (product - jnp.round(product * inverse) * length) * inverse
    square = turns * turns
    sine = jnp.float32(SIN_PI[-1])
    for term in SIN_PI[-2::-1]:
        sine = sine * square + term
    sine = sine * turns
    cosine = jnp.float32(COS_PI[-1])
    for term in COS_PI[-2::-1]:
        cosine = cosine * square + term
    return 1.0 - 2.0 * sine * sine, 2.0 * sine * cosine


def gather_rows(arrived, fields_ref, groups, waves):
    blocks = arrived.shape[0]
    full, rest, per_slot, _ = packing(waves, groups)
    for g in range(groups):
        pieces = [
            arrived[w, chunk * groups + g].astype(jnp.float32)
            for w in range(blocks)
            for chunk in range(full)
        ]
        if rest:
            slot, at = full * groups + g // per_slot, g % per_slot * rest
            ends = [arrived[w, slot].astype(jnp.float32) for w in range(blocks)]
            pieces += [end[:, at : at + rest] for end in ends]
        fields_ref[:, g, :] = jnp.concatenate(pieces, axis=1)


def tables_of(wave, length, inverse, table_ref):
    row = lax.broadcasted_iota(jnp.int32, (8, 1), 0).astype(jnp.float32)
    fine_cos, fine_sin = trig(wave, row, length, inverse)
    for top in range(LANES // 64):
        coarse_cos, coarse_sin = trig(wave, 64 * top + 8 * row, length, inverse)
        for pair in range(4):
            cosines, sines = [], []
            for a in (2 * pair, 2 * pair + 1):
                c, s = coarse_cos[a : a + 1], coarse_sin[a : a + 1]
                cosines.append(c * fine_cos - s * fine_sin)
                sines.append(-(s * fine_cos + c * fine_sin))
            at = 64 * top + 16 * pair
            table_ref[at : at + 16, 0:M] = jnp.concatenate(cosines, axis=0).astype(jnp.bfloat16)
            table_ref[at : at + 16, M : 2 * M] = jnp.concatenate(sines, axis=0).astype(jnp.bfloat16)


def synthesis(wave, count, columns, points, fields, table_ref, left_ref):
    length = count.astype(jnp.float32)
    inverse = 1.0 / length
    local = fields.shape[0] // 2
    rows = columns * local
    weight = jnp.where(wave == 0, 1.0, jnp.where(2 * wave < length, 2.0, 0.0))
    column = (lax.broadcasted_iota(jnp.int32, (rows, 1), 0) // local).astype(jnp.float32)
    cosine, sine = trig(wave, points * column, length, inverse)
    real = jnp.concatenate([fields[:local] * weight] * columns, axis=0)
    imag = jnp.concatenate([fields[local:] * weight] * columns, axis=0)
    real, imag = real * cosine - imag * sine, real * sine + imag * cosine
    row = lax.broadcasted_iota(jnp.int32, (8, 1), 0).astype(jnp.float32)
    for block in range(pl.cdiv(points, LANES)):
        if block % 8 == 0:
            block_cos, block_sin = trig(wave, LANES * (block + row), length, inverse)
        c = block_cos[block % 8 : block % 8 + 1]
        s = block_sin[block % 8 : block % 8 + 1]
        at = block * rows
        left_ref[at : at + rows, 0:M] = (real * c - imag * s).astype(jnp.bfloat16)
        left_ref[at : at + rows, M : 2 * M] = (real * s + imag * c).astype(jnp.bfloat16)
    return lax.dot_general(
        left_ref[...],
        table_ref[...],
        (((1,), (1,)), ((), ())),
        preferred_element_type=jnp.float32,
    )


def slot_latitude(i, lats, blocks):
    return jnp.where(lax.axis_index("wa") >= blocks // 2, lats - 1 - i, i)


def fourier_kernel(
    groups, points, points_ref, pairs_ref, sent, landed,
    arrived, fields_ref, tables_ref, left_ref, sums_ref, leaving,
    own_sem, send_band, recv_band, send_level, recv_level,
):
    lats = tables_ref.shape[0]
    columns, parts = landed.shape[:2]
    blocks = arrived.shape[0]
    local = groups // 2
    me, level = lax.axis_index("wa"), lax.axis_index("vert")
    barrier = pltpu.get_barrier_semaphore()

    def greet_band(d, carry):
        pl.semaphore_signal(
            barrier, inc=1, device_id=(lax.rem(me + d, blocks), level), device_id_type=MESH
        )
        return carry

    def greet_level(e, carry):
        pl.semaphore_signal(
            barrier, inc=1, device_id=(me, lax.rem(level + e, columns)), device_id_type=MESH
        )
        return carry

    lax.fori_loop(1, blocks, greet_band, 0)
    lax.fori_loop(1, columns, greet_level, 0)
    own = pltpu.make_async_copy(sent.at[me], arrived.at[me], own_sem.at[0])
    own.start()
    pl.semaphore_wait(barrier, blocks + columns - 2)

    def band_copy(d):
        target = lax.rem(me + d, blocks)
        return pltpu.make_async_remote_copy(
            src_ref=sent.at[target],
            dst_ref=arrived.at[me],
            send_sem=send_band.at[d],
            recv_sem=recv_band.at[d],
            device_id=(target, level),
            device_id_type=MESH,
        )

    def band_arrival(d):
        source = lax.rem(me + blocks - d, blocks)
        return pltpu.make_async_remote_copy(
            src_ref=sent.at[source],
            dst_ref=arrived.at[source],
            send_sem=send_band.at[d],
            recv_sem=recv_band.at[d],
            device_id=(source, level),
            device_id_type=MESH,
        )

    def level_copy(part, e):
        target = lax.rem(level + e, columns)
        return pltpu.make_async_remote_copy(
            src_ref=leaving.at[part, target],
            dst_ref=landed.at[level, part],
            send_sem=send_level.at[part, e],
            recv_sem=recv_level.at[part, e],
            device_id=(me, target),
            device_id_type=MESH,
        )

    def level_arrival(part, e):
        source = lax.rem(level + columns - e, columns)
        return pltpu.make_async_remote_copy(
            src_ref=leaving.at[part, source],
            dst_ref=landed.at[source, part],
            send_sem=send_level.at[part, e],
            recv_sem=recv_level.at[part, e],
            device_id=(me, source),
            device_id_type=MESH,
        )

    def start_band(d, carry):
        band_copy(d).start()
        return carry

    lax.fori_loop(1, blocks, start_band, 0)
    wave = packed_order(pairs_ref[...].astype(jnp.float32), blocks)

    def make_tables(i, carry):
        length = points_ref[slot_latitude(i, lats, blocks)].astype(jnp.float32)
        tables_of(wave, length, 1.0 / length, tables_ref.at[i])
        return carry

    lax.fori_loop(0, lats, make_tables, 0)
    own.wait()

    def finish_band(d, carry):
        band_arrival(d).wait_recv()
        band_copy(d).wait_send()
        return carry

    lax.fori_loop(1, blocks, finish_band, 0)
    gather_rows(arrived, fields_ref, groups, M // blocks)
    each = lats // parts
    rows = columns * local

    def one_part(part, carry):
        for j in range(each):
            i = part * each + j
            product = synthesis(
                wave,
                points_ref[slot_latitude(i, lats, blocks)],
                columns,
                points,
                fields_ref[i],
                tables_ref.at[i],
                left_ref,
            )
            for block in range(product.shape[0] // rows):
                for v in range(columns):
                    at = block * rows + v * local
                    sums_ref[v, j * local : (j + 1) * local, block * LANES : (block + 1) * LANES] = (
                        product[at : at + local]
                    )
        for v in range(columns):
            leaving[part, v] = sums_ref[v].astype(jnp.bfloat16)

        def start_level(e, inner):
            level_copy(part, e).start()
            return inner

        lax.fori_loop(1, columns, start_level, 0)
        pltpu.make_async_copy(
            leaving.at[part, level], landed.at[level, part], own_sem.at[1 + part]
        ).start()
        return carry

    lax.fori_loop(0, parts, one_part, 0)

    def finish_part(part, carry):
        def finish(e, inner):
            level_arrival(part, e).wait_recv()
            level_copy(part, e).wait_send()
            return inner

        pltpu.make_async_copy(
            leaving.at[part, level], landed.at[level, part], own_sem.at[1 + part]
        ).wait()
        return lax.fori_loop(1, columns, finish, carry)

    lax.fori_loop(0, parts, finish_part, 0)


def fourier_step(sent, pair_waves, points, points_device, groups, columns):
    blocks, slots, lats, _ = sent.shape
    local = groups // 2
    parts = 2
    chunks = pl.cdiv(points_device, LANES)
    rows = lats // parts * local
    return pl.pallas_call(
        functools.partial(fourier_kernel, groups, points_device),
        out_shape=jax.ShapeDtypeStruct((columns, parts, rows, chunks * LANES), jnp.bfloat16),
        in_specs=[
            pl.BlockSpec(memory_space=pltpu.SMEM),
            pl.BlockSpec(memory_space=pltpu.VMEM),
            pl.BlockSpec(memory_space=pl.ANY),
        ],
        out_specs=pl.BlockSpec(memory_space=pl.ANY),
        scratch_shapes=[
            pltpu.VMEM((blocks, slots, lats, LANES), jnp.bfloat16),
            pltpu.VMEM((lats, groups, M), jnp.float32),
            pltpu.VMEM((lats, LANES, 2 * M), jnp.bfloat16),
            pltpu.VMEM((chunks * columns * local, 2 * M), jnp.bfloat16),
            pltpu.VMEM((columns, rows, chunks * LANES), jnp.float32),
            pltpu.VMEM((parts, columns, rows, chunks * LANES), jnp.bfloat16),
            pltpu.SemaphoreType.DMA((1 + parts,)),
            pltpu.SemaphoreType.DMA((blocks,)),
            pltpu.SemaphoreType.DMA((blocks,)),
            pltpu.SemaphoreType.DMA((parts, columns)),
            pltpu.SemaphoreType.DMA((parts, columns)),
        ],
        compiler_params=pltpu.CompilerParams(collective_id=0, has_side_effects=True),
        name="fourier",
    )(points, pair_waves.reshape(1, -1), sent)


def place_kernel(blocks, points_ref, landed, out_ref):
    lats, fields, points = out_ref.shape
    columns, parts = landed.shape[:2]
    each, local = lats // parts, fields // columns
    first_point = lax.axis_index("vert") * points
    for part in range(parts):
        values = [landed[v, part].astype(jnp.float32) for v in range(columns)]
        for j in range(each):
            lat = slot_latitude(part * each + j, lats, blocks)
            rows = jnp.concatenate([value[j * local : (j + 1) * local] for value in values], axis=0)
            index = first_point + lax.broadcasted_iota(jnp.int32, rows.shape, 1)
            out_ref[lat] = jnp.where(index < points_ref[lat], rows, 0.0)[:, :points]


def place_step(landed, points, points_device, lats, fields, blocks):
    return pl.pallas_call(
        functools.partial(place_kernel, blocks),
        out_shape=jax.ShapeDtypeStruct((lats, fields, points_device), jnp.float32),
        in_specs=[
            pl.BlockSpec(memory_space=pltpu.SMEM),
            pl.BlockSpec(memory_space=pltpu.VMEM),
        ],
        out_specs=pl.BlockSpec(memory_space=pltpu.VMEM),
        name="place",
    )(points, landed)


def body(spectra, legendre, pair_waves, points):
    blocks, columns = lax.axis_size("wa"), lax.axis_size("vert")
    step_length = 8 * columns
    points_device = 8 * ((4 * M + 16 + step_length - 1) // step_length)
    groups = spectra.shape[1] * spectra.shape[2]
    sent = legendre_step(spectra, jnp.swapaxes(legendre, 1, 2), pair_waves, blocks)
    landed = fourier_step(sent, pair_waves, points, points_device, groups, columns)
    fields = columns * groups // 2
    return place_step(landed, points, points_device, points.shape[0], fields, blocks)


def solution(mesh):
    in_specs = (P("wa", None, "vert", None), P("wa", None, None), P(), P("wa"))
    out_specs = P("wa", None, "vert")
    return jax.shard_map(body, mesh=mesh, in_specs=in_specs, out_specs=out_specs, check_vma=False)
```

time: 36.4 us -> 30.6 us (0.84)
  local copies, waits for them, and re-layouts: 4 us -> 1.28 us
  Pallas kernels: 31.2 us -> 29 us
  other arithmetic: 0.68 us -> 0 us
    pallas_call x1 -> x2, Pallas kernels: 22.1 us -> 19.8 us  [the longest x1 18 us: fourier_step(): pl.pallas_call(functools.partial(fourier_kernel, groups, points_device),...]
    unnamed x1 -> x0, local copies, waits for them, and re-layouts: 1.74 us -> none
    dynamic_slice x1 -> x0, local copies, waits for them, and re-layouts: 1.35 us -> none  [body(): lax.dynamic_slice_in_dim(pair_waves, lax.axis_index('wa') * pair_count, p...]
    convert_element_type x1 -> x0, other arithmetic: 0.6 us -> none  [body(): waves = waves.reshape(1, -1).astype(jnp.float32)]
    reshape x1, local copies, waits for them, and re-layouts: 0.76 us -> 1.28 us  [fourier_step(): pair_waves.reshape(1, -1)]
where the time goes in v2:
time: 30.6 us; the launch traced here: 30.3 us
  Pallas kernels  29 us (95%)
  local copies, waits for them, and re-layouts  1.28 us (4%)
    pallas_call x1, Pallas kernels, fourier_step(): pl.pallas_call(functools.partial(fourier_kernel, groups, points_device),...  18 us
    pallas_call x1, Pallas kernels, legendre_step(): pl.pallas_call(functools.partial(legendre_kernel, block), out_shape=jax.S...  9.24 us
    pallas_call x1, Pallas kernels, place_step(): pl.pallas_call(functools.partial(place_kernel, blocks), out_shape=jax.Sha...  1.78 us
    reshape x1, local copies, waits for them, and re-layouts, fourier_step(): pair_waves.reshape(1, -1)  1.28 us

profile of v2, /device:TPU:0, one launch (start us, length us, event | category | flops | bytes accessed | tf_op | source)
XLA Modules:
  0.0 30.3 jit_solution(4650280451943225431)
XLA Ops:
  0.0 1.3 %reshape.3.pairs_ref = s32[1,640]{1,0:T(1,128)} reshape(s32[640]{0:T(1024)} %waves_ref.1) | data formatting | bytes 5120 | tf_op jit(solution)/shard_map/reshape | solution.py:390
  1.3 9.2 %legendre.1.sent = bf16[8,5,8,128]{3,2,1,0:T(8,128)(2,1)} custom-call(s32[640]{0:T(1024)} %waves_ref.1, bf16[80,2,2,1288]{3,2,1,0:T(2,128)(2,1)} %spectra_ref.1, bf16[80,32,1288]{2,1,0:T(8,128)(2,1)} %bitcast.1), custom_call_target="tpu_custom_call" | custom-call | tf_op jit(solution)/shard_map/legendre/pallas_call | solution.py:119
  10.5 18.0 %fourier.1.landed = bf16[4,2,8,1408]{3,2,1,0:T(8,128)(2,1)} custom-call(s32[8]{0:T(128)} %points_ref.3, s32[1,640]{1,0:T(1,128)} %reshape.3.pairs_ref, bf16[8,5,8,128]{3,2,1,0:T(8,128)(2,1)} %legendre.1.sent), custom_call_target="tpu_custom_call" | custom-call | tf_op jit(solution)/shard_map/fourier/pallas_call | solution.py:366
  28.5 1.8 %place.1 = f32[8,8,1288]{2,1,0:T(8,128)} custom-call(s32[8]{0:T(128)} %points_ref.3, bf16[4,2,8,1408]{3,2,1,0:T(8,128)(2,1)} %fourier.1.landed), custom_call_target="tpu_custom_call" | custom-call | tf_op jit(solution)/shard_map/place/pallas_call | solution.py:408

commit v3 on v2

--- a/solution.py
+++ b/solution.py
@@ -1,5 +1,4 @@
 import functools
-import math
 
 import jax
 import jax.numpy as jnp
@@ -11,25 +10,8 @@
 M = 1280
 LANES = 128
 MESH = pl.DeviceIdType.MESH
-SIN_PI = (
-    math.pi,
-    -math.pi**3 / 6,
-    math.pi**5 / 120,
-    -math.pi**7 / 5040,
-    math.pi**9 / 362880,
-    -math.pi**11 / 39916800,
-    math.pi**13 / 6227020800,
-)
-
-COS_PI = (
-    1.0,
-    -math.pi**2 / 2,
-    math.pi**4 / 24,
-    -math.pi**6 / 720,
-    math.pi**8 / 40320,
-    -math.pi**10 / 3628800,
-    math.pi**12 / 479001600,
-)
+SIN_PI = (3.141592640183955, -5.167710090327305, 2.5500776596396157, -0.5982921588969844, 0.07765940708214343)
+COS_PI = (0.9999999534665123, -4.934792858655412, 4.058411913769657, -1.3318801587031317, 0.21969679350917085)
 
 
 def packing(waves, groups):
@@ -51,26 +33,35 @@
     return jnp.concatenate(heads + tails, axis=1)
 
 
-def legendre_kernel(pair_block, waves_ref, spectra_ref, legendre_ref, out_ref, scratch):
+def legendre_kernel(pair_block, waves_ref, spectra_ref, legendre_ref, out_ref, scratch, patterns):
     step = pl.program_id(0)
     parts, fields, padded = spectra_ref.shape[1:]
     half = parts * fields
     heights = legendre_ref.shape[1]
     num_pairs = scratch.shape[0]
-    shape = (2 * half, padded)
-    column = lax.broadcasted_iota(jnp.int32, shape, 1)
-    plain = lax.broadcasted_iota(jnp.int32, shape, 0) < half
-    alternating = jnp.where(plain | (column % 2 == 0), 1.0, -1.0)
+    column = lax.broadcasted_iota(jnp.int32, (8, padded), 1)
+    row = lax.broadcasted_iota(jnp.int32, (8, padded), 0)
+
+    @pl.when(step == 0)
+    def _():
+        later = (row // 2) % 2 == 1
+        signed = row % 2 == 1
+        plain = jnp.where(signed & (column % 2 == 1), -1.0, 1.0)
+        even = jnp.where(later & (column < M + 1), plain, 0.0)
+        patterns[0] = jnp.where(later, 0.0, plain)
+        patterns[1] = even
+        patterns[2] = jnp.where(signed, -even, even)
+
     for i in range(pair_block):
         pair = step * pair_block + i
         boundary = M - waves_ref[lax.axis_index("wa") * num_pairs + pair]
-        flip = jnp.where(boundary % 2 == 0, 1.0, -1.0)
-        rows = [spectra_ref[i, part].astype(jnp.float32) for part in range(parts)]
-        signed = jnp.concatenate(rows + rows, axis=0) * alternating
-        first = jnp.where(column < boundary, signed, 0.0)
-        second = jnp.where((column >= boundary) & (column < M + 1), signed, 0.0)
-        second = second * jnp.where(plain, 1.0, flip)
-        masked = jnp.concatenate([first, second], axis=0).astype(jnp.bfloat16)
+        pattern = jnp.where(column < boundary, patterns[0], patterns[1 + boundary % 2])
+        masked = []
+        for part in range(parts):
+            rows = spectra_ref[i, part].astype(jnp.float32)
+            for at in range(0, fields, 2):
+                masked.append(jnp.where(row < 4, rows[at : at + 1], rows[at + 1 : at + 2]) * pattern)
+        masked = jnp.concatenate(masked, axis=0).astype(jnp.bfloat16)
         scratch[pair, :, 0:heights] = lax.dot_general(
             masked,
             legendre_ref[i],
@@ -84,10 +75,10 @@
         full, rest, per_slot, _ = packing(2 * scratch.shape[0], half)
         for sign in range(2):
             rows = []
-            for row in range(half):
+            for coefficient in range(half):
                 halves = []
                 for part in range(2):
-                    picked = scratch[:, (part * 2 + sign) * half + row, :]
+                    picked = scratch[:, 4 * coefficient + 2 * part + sign, :]
                     halves.append(jnp.transpose(picked)[:heights])
                 rows.append(jnp.concatenate(halves, axis=1))
             slots = [
@@ -127,7 +118,8 @@
         ],
         out_specs=pl.BlockSpec(result, lambda i: (0, 0, 0, 0)),
         scratch_shapes=[
-            pltpu.VMEM((pairs, 4 * parts * fields, max(heights, LANES)), jnp.float32)
+            pltpu.VMEM((pairs, 4 * parts * fields, max(heights, LANES)), jnp.float32),
+            pltpu.VMEM((3, 8, padded), jnp.float32),
         ],
         name="legendre",
     )(pair_waves, spectra, legendre)
@@ -144,7 +136,8 @@
     cosine = jnp.float32(COS_PI[-1])
     for term in COS_PI[-2::-1]:
         cosine = cosine * square + term
-    return 1.0 - 2.0 * sine * sine, 2.0 * sine * cosine
+    double = sine + sine
+    return 1.0 - double * sine, double * cosine
 
 
 def gather_rows(arrived, fields_ref, groups, waves):
@@ -163,11 +156,20 @@
         fields_ref[:, g, :] = jnp.concatenate(pieces, axis=1)
 
 
+def doubled_shift(cosine, sine):
+    c, s = cosine[4:5], sine[4:5]
+    c, s = 1.0 - 2.0 * s * s, 2.0 * s * c
+    return cosine * c - sine * s, sine * c + cosine * s
+
+
 def tables_of(wave, length, inverse, table_ref):
     row = lax.broadcasted_iota(jnp.int32, (8, 1), 0).astype(jnp.float32)
     fine_cos, fine_sin = trig(wave, row, length, inverse)
     for top in range(LANES // 64):
-        coarse_cos, coarse_sin = trig(wave, 64 * top + 8 * row, length, inverse)
+        if top == 0:
+            coarse_cos, coarse_sin = trig(wave, 8 * row, length, inverse)
+        else:
+            coarse_cos, coarse_sin = doubled_shift(coarse_cos, coarse_sin)
         for pair in range(4):
             cosines, sines = [], []
             for a in (2 * pair, 2 * pair + 1):
@@ -192,7 +194,11 @@
     real, imag = real * cosine - imag * sine, real * sine + imag * cosine
     row = lax.broadcasted_iota(jnp.int32, (8, 1), 0).astype(jnp.float32)
     for block in range(pl.cdiv(points, LANES)):
-        if block % 8 == 0:
+        if block == 0:
+            block_cos, block_sin = trig(wave, LANES * row, length, inverse)
+        elif block == 8:
+            block_cos, block_sin = doubled_shift(block_cos, block_sin)
+        elif block % 8 == 0:
             block_cos, block_sin = trig(wave, LANES * (block + row), length, inverse)
         c = block_cos[block % 8 : block % 8 + 1]
         s = block_sin[block % 8 : block % 8 + 1]
@@ -239,7 +245,6 @@
     lax.fori_loop(1, columns, greet_level, 0)
     own = pltpu.make_async_copy(sent.at[me], arrived.at[me], own_sem.at[0])
     own.start()
-    pl.semaphore_wait(barrier, blocks + columns - 2)
 
     def band_copy(d):
         target = lax.rem(me + d, blocks)
@@ -289,15 +294,18 @@
         band_copy(d).start()
         return carry
 
-    lax.fori_loop(1, blocks, start_band, 0)
-    wave = packed_order(pairs_ref[...].astype(jnp.float32), blocks)
+    wave = packed_order(pairs_ref[...].astype(jnp.float32).reshape(1, -1), blocks)
 
     def make_tables(i, carry):
         length = points_ref[slot_latitude(i, lats, blocks)].astype(jnp.float32)
         tables_of(wave, length, 1.0 / length, tables_ref.at[i])
         return carry
 
-    lax.fori_loop(0, lats, make_tables, 0)
+    early = lats // 4
+    lax.fori_loop(0, early, make_tables, 0)
+    pl.semaphore_wait(barrier, blocks + columns - 2)
+    lax.fori_loop(1, blocks, start_band, 0)
+    lax.fori_loop(early, lats, make_tables, 0)
     own.wait()
 
     def finish_band(d, carry):
@@ -387,7 +395,7 @@
         ],
         compiler_params=pltpu.CompilerParams(collective_id=0, has_side_effects=True),
         name="fourier",
-    )(points, pair_waves.reshape(1, -1), sent)
+    )(points, pair_waves, sent)
 
 
 def place_kernel(blocks, points_ref, landed, out_ref):

time: 30.6 us -> 28.8 us (0.941)
  local copies, waits for them, and re-layouts: 1.28 us -> 0 us
  Pallas kernels: 29 us -> 28.5 us
    reshape x1 -> x0, local copies, waits for them, and re-layouts: 1.28 us -> none  [fourier_step(): pair_waves.reshape(1, -1)]
    pallas_call x1, Pallas kernels: 18 us -> 17.4 us  [fourier_step(): pl.pallas_call(functools.partial(fourier_kernel, groups, points_device),...]
where the time goes in v3:
time: 28.8 us; the launch traced here: 28.5 us
  Pallas kernels  28.5 us (99%)
    pallas_call x1, Pallas kernels, fourier_step(): pl.pallas_call(functools.partial(fourier_kernel, groups, points_device),...  17.4 us
    pallas_call x1, Pallas kernels, legendre_step(): pl.pallas_call(functools.partial(legendre_kernel, block), out_shape=jax.S...  9.28 us
    pallas_call x1, Pallas kernels, place_step(): pl.pallas_call(functools.partial(place_kernel, blocks), out_shape=jax.Sha...  1.78 us

profile of v3, /device:TPU:0, one launch (start us, length us, event | category | flops | bytes accessed | tf_op | source)
XLA Modules:
  0.0 28.5 jit_solution(6385481223128229679)
XLA Ops:
  0.0 9.3 %legendre.1.sent = bf16[8,5,8,128]{3,2,1,0:T(8,128)(2,1)} custom-call(s32[640]{0:T(1024)} %pairs_ref.1, bf16[80,2,2,1288]{3,2,1,0:T(2,128)(2,1)} %spectra_ref.1, bf16[80,32,1288]{2,1,0:T(8,128)(2,1)} %bitcast.1), custom_call_target="tpu_custom_call" | custom-call | tf_op jit(solution)/shard_map/legendre/pallas_call | solution.py:110
  9.3 17.4 %fourier.1.landed = bf16[4,2,8,1408]{3,2,1,0:T(8,128)(2,1)} custom-call(s32[8]{0:T(128)} %points_ref.3, s32[640]{0:T(1024)} %pairs_ref.1, bf16[8,5,8,128]{3,2,1,0:T(8,128)(2,1)} %legendre.1.sent), custom_call_target="tpu_custom_call" | custom-call | tf_op jit(solution)/shard_map/fourier/pallas_call | solution.py:374
  26.7 1.8 %place.1 = f32[8,8,1288]{2,1,0:T(8,128)} custom-call(s32[8]{0:T(128)} %points_ref.3, bf16[4,2,8,1408]{3,2,1,0:T(8,128)(2,1)} %fourier.1.landed), custom_call_target="tpu_custom_call" | custom-call | tf_op jit(solution)/shard_map/place/pallas_call | solution.py:416

commit v4 on v3

--- a/solution.py
+++ b/solution.py
@@ -33,8 +33,10 @@
     return jnp.concatenate(heads + tails, axis=1)
 
 
-def legendre_kernel(pair_block, waves_ref, spectra_ref, legendre_ref, out_ref, scratch, patterns):
-    step = pl.program_id(0)
+def legendre_kernel(
+    pair_block, waves_ref, spectra, legendre, out_ref,
+    scratch, patterns, spectra_ref, legendre_ref, sems,
+):
     parts, fields, padded = spectra_ref.shape[1:]
     half = parts * fields
     heights = legendre_ref.shape[1]
@@ -42,62 +44,79 @@
     column = lax.broadcasted_iota(jnp.int32, (8, padded), 1)
     row = lax.broadcasted_iota(jnp.int32, (8, padded), 0)
 
-    @pl.when(step == 0)
-    def _():
-        later = (row // 2) % 2 == 1
-        signed = row % 2 == 1
-        plain = jnp.where(signed & (column % 2 == 1), -1.0, 1.0)
-        even = jnp.where(later & (column < M + 1), plain, 0.0)
-        patterns[0] = jnp.where(later, 0.0, plain)
-        patterns[1] = even
-        patterns[2] = jnp.where(signed, -even, even)
-
-    for i in range(pair_block):
-        pair = step * pair_block + i
-        boundary = M - waves_ref[lax.axis_index("wa") * num_pairs + pair]
-        pattern = jnp.where(column < boundary, patterns[0], patterns[1 + boundary % 2])
-        masked = []
-        for part in range(parts):
-            rows = spectra_ref[i, part].astype(jnp.float32)
-            for at in range(0, fields, 2):
-                masked.append(jnp.where(row < 4, rows[at : at + 1], rows[at + 1 : at + 2]) * pattern)
-        masked = jnp.concatenate(masked, axis=0).astype(jnp.bfloat16)
-        scratch[pair, :, 0:heights] = lax.dot_general(
-            masked,
-            legendre_ref[i],
-            (((1,), (1,)), ((), ())),
-            preferred_element_type=jnp.float32,
-        )
-
-    @pl.when(step == pl.num_programs(0) - 1)
-    def _():
-        blocks, _, lats, _ = out_ref.shape
-        full, rest, per_slot, _ = packing(2 * scratch.shape[0], half)
-        for sign in range(2):
-            rows = []
-            for coefficient in range(half):
-                halves = []
-                for part in range(2):
-                    picked = scratch[:, 4 * coefficient + 2 * part + sign, :]
-                    halves.append(jnp.transpose(picked)[:heights])
-                rows.append(jnp.concatenate(halves, axis=1))
-            slots = [
-                rows[row][:, chunk * LANES : (chunk + 1) * LANES]
-                for chunk in range(full)
-                for row in range(half)
-            ]
-            if rest:
-                for at in range(0, half, per_slot):
-                    pieces = [row[:, full * LANES :] for row in rows[at : at + per_slot]]
-                    spare = LANES - rest * len(pieces)
-                    if spare:
-                        pieces.append(jnp.zeros((heights, spare), jnp.float32))
-                    slots.append(jnp.concatenate(pieces, axis=1))
-            for slot, values in enumerate(slots):
-                values = values.astype(jnp.bfloat16)
-                for b in range(blocks // 2):
-                    target = b if sign == 0 else blocks - 1 - b
-                    out_ref[target, slot] = values[b * lats : (b + 1) * lats]
+    def copies(step):
+        at = pl.ds(step * pair_block, pair_block)
+        return (
+            pltpu.make_async_copy(spectra.at[at], spectra_ref.at[at], sems.at[0, step]),
+            pltpu.make_async_copy(legendre.at[at], legendre_ref.at[at], sems.at[1, step]),
+        )
+
+    def start(step, carry):
+        for copy in copies(step):
+            copy.start()
+        return carry
+
+    steps = num_pairs // pair_block
+    lax.fori_loop(0, steps, start, 0)
+
+    later = (row // 2) % 2 == 1
+    signed = row % 2 == 1
+    plain = jnp.where(signed & (column % 2 == 1), -1.0, 1.0)
+    even = jnp.where(later & (column < M + 1), plain, 0.0)
+    patterns[0] = jnp.where(later, 0.0, plain)
+    patterns[1] = even
+    patterns[2] = jnp.where(signed, -even, even)
+
+    def project(step, carry):
+        for copy in copies(step):
+            copy.wait()
+        for i in range(pair_block):
+            pair = step * pair_block + i
+            boundary = M - waves_ref[lax.axis_index("wa") * num_pairs + pair]
+            pattern = jnp.where(column < boundary, patterns[0], patterns[1 + boundary % 2])
+            masked = []
+            for part in range(parts):
+                rows = spectra_ref[pair, part].astype(jnp.float32)
+                for at in range(0, fields, 2):
+                    picked = jnp.where(row < 4, rows[at : at + 1], rows[at + 1 : at + 2])
+                    masked.append(picked * pattern)
+            masked = jnp.concatenate(masked, axis=0).astype(jnp.bfloat16)
+            scratch[pair, :, 0:heights] = lax.dot_general(
+                masked,
+                legendre_ref[pair],
+                (((1,), (1,)), ((), ())),
+                preferred_element_type=jnp.float32,
+            )
+        return carry
+
+    lax.fori_loop(0, steps, project, 0)
+    blocks, _, lats, _ = out_ref.shape
+    full, rest, per_slot, _ = packing(2 * scratch.shape[0], half)
+    for sign in range(2):
+        rows = []
+        for coefficient in range(half):
+            halves = []
+            for part in range(2):
+                picked = scratch[:, 4 * coefficient + 2 * part + sign, :]
+                halves.append(jnp.transpose(picked)[:heights])
+            rows.append(jnp.concatenate(halves, axis=1))
+        slots = [
+            rows[row][:, chunk * LANES : (chunk + 1) * LANES]
+            for chunk in range(full)
+            for row in range(half)
+        ]
+        if rest:
+            for at in range(0, half, per_slot):
+                pieces = [row[:, full * LANES :] for row in rows[at : at + per_slot]]
+                spare = LANES - rest * len(pieces)
+                if spare:
+                    pieces.append(jnp.zeros((heights, spare), jnp.float32))
+                slots.append(jnp.concatenate(pieces, axis=1))
+        for slot, values in enumerate(slots):
+            values = values.astype(jnp.bfloat16)
+            for b in range(blocks // 2):
+                target = b if sign == 0 else blocks - 1 - b
+                out_ref[target, slot] = values[b * lats : (b + 1) * lats]
 
 
 def legendre_step(spectra, legendre, pair_waves, blocks):
@@ -110,16 +129,18 @@
     return pl.pallas_call(
         functools.partial(legendre_kernel, block),
         out_shape=jax.ShapeDtypeStruct(result, jnp.bfloat16),
-        grid=(pairs // block,),
         in_specs=[
             pl.BlockSpec(memory_space=pltpu.SMEM),
-            pl.BlockSpec((block, parts, fields, padded), lambda i: (i, 0, 0, 0)),
-            pl.BlockSpec((block, heights, padded), lambda i: (i, 0, 0)),
+            pl.BlockSpec(memory_space=pl.ANY),
+            pl.BlockSpec(memory_space=pl.ANY),
         ],
-        out_specs=pl.BlockSpec(result, lambda i: (0, 0, 0, 0)),
+        out_specs=pl.BlockSpec(memory_space=pltpu.VMEM),
         scratch_shapes=[
             pltpu.VMEM((pairs, 4 * parts * fields, max(heights, LANES)), jnp.float32),
             pltpu.VMEM((3, 8, padded), jnp.float32),
+            pltpu.VMEM(spectra.shape, spectra.dtype),
+            pltpu.VMEM(legendre.shape, legendre.dtype),
+            pltpu.SemaphoreType.DMA((2, pairs // block)),
         ],
         name="legendre",
     )(pair_waves, spectra, legendre)
@@ -165,6 +186,7 @@
 def tables_of(wave, length, inverse, table_ref):
     row = lax.broadcasted_iota(jnp.int32, (8, 1), 0).astype(jnp.float32)
     fine_cos, fine_sin = trig(wave, row, length, inverse)
+    fine_neg = -fine_cos
     for top in range(LANES // 64):
         if top == 0:
             coarse_cos, coarse_sin = trig(wave, 8 * row, length, inverse)
@@ -175,7 +197,7 @@
             for a in (2 * pair, 2 * pair + 1):
                 c, s = coarse_cos[a : a + 1], coarse_sin[a : a + 1]
                 cosines.append(c * fine_cos - s * fine_sin)
-                sines.append(-(s * fine_cos + c * fine_sin))
+                sines.append(s * fine_neg - c * fine_sin)
             at = 64 * top + 16 * pair
             table_ref[at : at + 16, 0:M] = jnp.concatenate(cosines, axis=0).astype(jnp.bfloat16)
             table_ref[at : at + 16, M : 2 * M] = jnp.concatenate(sines, axis=0).astype(jnp.bfloat16)

time: 28.8 us -> 26.1 us (0.906)
  Pallas kernels: 28.5 us -> 25.9 us
    pallas_call x1, Pallas kernels: 9.28 us -> 6.68 us  [legendre_step(): pl.pallas_call(functools.partial(legendre_kernel, block), out_shape=jax.S...]
where the time goes in v4:
time: 26.1 us; the launch traced here: 25.9 us
  Pallas kernels  25.9 us (99%)
    pallas_call x1, Pallas kernels, fourier_step(): pl.pallas_call(functools.partial(fourier_kernel, groups, points_device),...  17.4 us
    pallas_call x1, Pallas kernels, legendre_step(): pl.pallas_call(functools.partial(legendre_kernel, block), out_shape=jax.S...  6.68 us
    pallas_call x1, Pallas kernels, place_step(): pl.pallas_call(functools.partial(place_kernel, blocks), out_shape=jax.Sha...  1.78 us

profile of v4, /device:TPU:0, one launch (start us, length us, event | category | flops | bytes accessed | tf_op | source)
XLA Modules:
  0.0 25.9 jit_solution(1609704125949866607)
XLA Ops:
  0.0 6.7 %legendre.1.sent = bf16[8,5,8,128]{3,2,1,0:T(8,128)(2,1)} custom-call(s32[640]{0:T(1024)} %pairs_ref.1, bf16[80,2,2,1288]{3,2,1,0:T(2,128)(2,1)} %spectra.1, bf16[80,32,1288]{2,1,0:T(8,128)(2,1)} %bitcast.1), custom_call_target="tpu_custom_call" | custom-call | tf_op jit(solution)/shard_map/legendre/pallas_call | solution.py:129
  6.7 17.4 %fourier.1.landed = bf16[4,2,8,1408]{3,2,1,0:T(8,128)(2,1)} custom-call(s32[8]{0:T(128)} %points_ref.3, s32[640]{0:T(1024)} %pairs_ref.1, bf16[8,5,8,128]{3,2,1,0:T(8,128)(2,1)} %legendre.1.sent), custom_call_target="tpu_custom_call" | custom-call | tf_op jit(solution)/shard_map/fourier/pallas_call | solution.py:396
  24.1 1.8 %place.1 = f32[8,8,1288]{2,1,0:T(8,128)} custom-call(s32[8]{0:T(128)} %points_ref.3, bf16[4,2,8,1408]{3,2,1,0:T(8,128)(2,1)} %fourier.1.landed), custom_call_target="tpu_custom_call" | custom-call | tf_op jit(solution)/shard_map/place/pallas_call | solution.py:438

commit v5 on v4

--- a/solution.py
+++ b/solution.py
@@ -183,7 +183,7 @@
     return cosine * c - sine * s, sine * c + cosine * s
 
 
-def tables_of(wave, length, inverse, table_ref):
+def tables_of(wave, length, inverse, table_ref, turns_ref):
     row = lax.broadcasted_iota(jnp.int32, (8, 1), 0).astype(jnp.float32)
     fine_cos, fine_sin = trig(wave, row, length, inverse)
     fine_neg = -fine_cos
@@ -192,10 +192,13 @@
             coarse_cos, coarse_sin = trig(wave, 8 * row, length, inverse)
         else:
             coarse_cos, coarse_sin = doubled_shift(coarse_cos, coarse_sin)
+        turns_ref[0, 8 * top : 8 * top + 8] = coarse_cos
+        turns_ref[1, 8 * top : 8 * top + 8] = coarse_sin
         for pair in range(4):
             cosines, sines = [], []
             for a in (2 * pair, 2 * pair + 1):
-                c, s = coarse_cos[a : a + 1], coarse_sin[a : a + 1]
+                c = turns_ref[0, pl.ds(8 * top + a, 8, stride=0), :]
+                s = turns_ref[1, pl.ds(8 * top + a, 8, stride=0), :]
                 cosines.append(c * fine_cos - s * fine_sin)
                 sines.append(s * fine_neg - c * fine_sin)
             at = 64 * top + 16 * pair
@@ -241,7 +244,7 @@
 
 def fourier_kernel(
     groups, points, points_ref, pairs_ref, sent, landed,
-    arrived, fields_ref, tables_ref, left_ref, sums_ref, leaving,
+    arrived, fields_ref, tables_ref, turns_ref, left_ref, sums_ref, leaving,
     own_sem, send_band, recv_band, send_level, recv_level,
 ):
     lats = tables_ref.shape[0]
@@ -320,7 +323,7 @@
 
     def make_tables(i, carry):
         length = points_ref[slot_latitude(i, lats, blocks)].astype(jnp.float32)
-        tables_of(wave, length, 1.0 / length, tables_ref.at[i])
+        tables_of(wave, length, 1.0 / length, tables_ref.at[i], turns_ref)
         return carry
 
     early = lats // 4
@@ -406,6 +409,7 @@
             pltpu.VMEM((blocks, slots, lats, LANES), jnp.bfloat16),
             pltpu.VMEM((lats, groups, M), jnp.float32),
             pltpu.VMEM((lats, LANES, 2 * M), jnp.bfloat16),
+            pltpu.VMEM((2, LANES // 8, M), jnp.float32),
             pltpu.VMEM((chunks * columns * local, 2 * M), jnp.bfloat16),
             pltpu.VMEM((columns, rows, chunks * LANES), jnp.float32),
             pltpu.VMEM((parts, columns, rows, chunks * LANES), jnp.bfloat16),

time: 26.1 us -> 26.1 us (level)
  no operation moved by 1% of the time
where the time goes in v5:
time: 26.1 us; the launch traced here: 25.9 us
  Pallas kernels  25.9 us (99%)
    pallas_call x1, Pallas kernels, fourier_step(): pl.pallas_call(functools.partial(fourier_kernel, groups, points_device),...  17.4 us
    pallas_call x1, Pallas kernels, legendre_step(): pl.pallas_call(functools.partial(legendre_kernel, block), out_shape=jax.S...  6.68 us
    pallas_call x1, Pallas kernels, place_step(): pl.pallas_call(functools.partial(place_kernel, blocks), out_shape=jax.Sha...  1.78 us

profile of v5, /device:TPU:0, one launch (start us, length us, event | category | flops | bytes accessed | tf_op | source)
XLA Modules:
  0.0 25.9 jit_solution(8407017514585897517)
XLA Ops:
  0.0 6.7 %legendre.1.sent = bf16[8,5,8,128]{3,2,1,0:T(8,128)(2,1)} custom-call(s32[640]{0:T(1024)} %pairs_ref.1, bf16[80,2,2,1288]{3,2,1,0:T(2,128)(2,1)} %spectra.1, bf16[80,32,1288]{2,1,0:T(8,128)(2,1)} %bitcast.1), custom_call_target="tpu_custom_call" | custom-call | tf_op jit(solution)/shard_map/legendre/pallas_call | solution.py:129
  6.7 17.4 %fourier.1.landed = bf16[4,2,8,1408]{3,2,1,0:T(8,128)(2,1)} custom-call(s32[8]{0:T(128)} %points_ref.3, s32[640]{0:T(1024)} %pairs_ref.1, bf16[8,5,8,128]{3,2,1,0:T(8,128)(2,1)} %legendre.1.sent), custom_call_target="tpu_custom_call" | custom-call | tf_op jit(solution)/shard_map/fourier/pallas_call | solution.py:399
  24.1 1.8 %place.1 = f32[8,8,1288]{2,1,0:T(8,128)} custom-call(s32[8]{0:T(128)} %points_ref.3, bf16[4,2,8,1408]{3,2,1,0:T(8,128)(2,1)} %fourier.1.landed), custom_call_target="tpu_custom_call" | custom-call | tf_op jit(solution)/shard_map/place/pallas_call | solution.py:442
